TPU v7x, 32 devices: a whole 2x2x4 slice. The times are simulated.
32 devices in a mesh: design: 2 (over x), tile: 8 (over z, y), mode: 2 (over core).
Axes of the slice: x: 2, y: 2, z: 4, core: 2. Of those that a mesh axis runs over, the one named last changes fastest.
Arguments:
- forward: bfloat16 [4, 2, 4096, 4096], P(('design', 'mode'), None, 'tile'), parts along dimension 0, may hold values from -6 to 6
- adjoint_next: bfloat16 [4, 2, 4096, 4096], P(('design', 'mode'), None, 'tile'), parts along dimension 0, may hold values from -6 to 6
- phase: float32 [8192, 4096], P(('design', 'tile'), 'mode'), parts along dimension 0, may hold values from -3.140625 to 3.140625
- blocks: bfloat16 [2, 128, 4, 64, 64], P(None, 'design'), parts along dimension 1, may hold values from -0.25 to 0.25
- offsets: int32 [128, 4], P('design'), parts along dimension 0, may hold values from -2 to 2, as said below
Outputs:
- phase_next: float32 [8192, 4096], P(('design', 'tile'), 'mode'), parts along dimension 0
- forward_next: bfloat16 [4, 2, 4096, 4096], P(('design', 'mode'), None, 'tile'), parts along dimension 0
There are 2 independent parts, one for each index of `design`. A program takes and returns all parts, laid end to end along the dimension named above; each array names one. Nothing has to cross between parts.
Inputs may be any that keep to these rules, and one draw needn't show every extreme that they name: Each row of offsets holds 4 different values, all of -2 to 2 but one; row 0 holds both -2 and 2.
All inputs are finite; a program needn't handle non-finite values.
Results may differ from a plain program's by a relative error of at most 0.02.
Values may be sent and summed in bfloat16 or wider, within the bound.
A program may use at most 256 MiB of HBM per device.

v0:
```python
import jax
import jax.numpy as jnp
from jax import lax
from jax.sharding import PartitionSpec as P

BLK = 64
RADIUS = 2


def dense_operator(blocks_re, blocks_im, shifts, in_blocks):
    out_blocks = shifts.shape[0]
    block_size = blocks_re.shape[-1]
    picks = (
        jnp.arange(out_blocks, dtype=jnp.int32)[:, None, None] + shifts[:, :, None] + RADIUS
        == jnp.arange(in_blocks, dtype=jnp.int32)[None, None, :]
    ).astype(jnp.bfloat16)
    wide_re = jnp.einsum(
        "okb,okij->oibj", picks, blocks_re, preferred_element_type=jnp.float32
    ).astype(jnp.bfloat16)
    wide_im = jnp.einsum(
        "okb,okij->oibj", picks, blocks_im, preferred_element_type=jnp.float32
    ).astype(jnp.bfloat16)
    wide_re = wide_re.reshape(out_blocks * block_size, in_blocks * block_size)
    wide_im = wide_im.reshape(out_blocks * block_size, in_blocks * block_size)
    upper = jnp.stack([wide_re, -wide_im], axis=1)
    lower = jnp.stack([wide_im, wide_re], axis=1)
    return jnp.stack([upper, lower], axis=0)


def column_pass(field_in, operators):
    margin = RADIUS * BLK
    padded = jnp.pad(field_in, ((0, 0), (0, 0), (0, 0), (margin, margin)))
    results = []
    for group, operator in enumerate(operators):
        width_out = operator.shape[1]
        width_in = operator.shape[3]
        window = lax.slice_in_dim(padded, group * width_out, group * width_out + width_in, axis=3)
        results.append(
            jnp.einsum(
                "mprj,qipj->mqri", window, operator, preferred_element_type=jnp.float32
            ).astype(jnp.bfloat16)
        )
    return jnp.concatenate(results, axis=3)


def whole_row_pass(field_in, operators):
    margin = RADIUS * BLK
    padded = jnp.pad(field_in, ((0, 0), (0, 0), (margin, margin), (0, 0)))
    results = []
    for group, operator in enumerate(operators):
        width_out = operator.shape[1]
        width_in = operator.shape[3]
        window = lax.slice_in_dim(padded, group * width_out, group * width_out + width_in, axis=2)
        results.append(
            jnp.einsum(
                "mpjw,qipj->mqiw", window, operator, preferred_element_type=jnp.float32
            ).astype(jnp.bfloat16)
        )
    return jnp.concatenate(results, axis=2)


def row_pass(middle, operators):
    columns = lax.all_to_all(middle, "tile", split_axis=3, concat_axis=2, tiled=True)
    finished = whole_row_pass(columns, operators)
    return lax.all_to_all(finished, "tile", split_axis=2, concat_axis=3, tiled=True)


def body(forward, adjoint_next, phase, blocks, offsets):
    block_total = offsets.shape[0]
    raw_index = jnp.arange(block_total, dtype=jnp.int32)[:, None] + offsets
    inside = (raw_index >= 0) & (raw_index < block_total)
    zero_block = jnp.zeros((), blocks.dtype)
    real_all = jnp.where(inside[:, :, None, None], blocks[0], zero_block)
    imag_all = jnp.where(inside[:, :, None, None], blocks[1], zero_block)
    group_blocks = 8
    operators = []
    for group in range(block_total // group_blocks):
        low = group * group_blocks
        operators.append(
            dense_operator(
                real_all[low : low + group_blocks],
                imag_all[low : low + group_blocks],
                offsets[low : low + group_blocks],
                group_blocks + 2 * RADIUS,
            )
        )
    full_phase = lax.all_gather(phase, "mode", axis=1, tiled=True)
    cos_old = jnp.cos(full_phase)
    sin_old = jnp.sin(full_phase)
    conj_next = jnp.stack([adjoint_next[:, 0], -adjoint_next[:, 1]], axis=1)
    back_middle = column_pass(conj_next, operators)
    conj_here = row_pass(back_middle, operators)
    fwd_real = forward[:, 0].astype(jnp.float32)
    fwd_imag = forward[:, 1].astype(jnp.float32)
    cj_real = conj_here[:, 0].astype(jnp.float32)
    cj_imag = conj_here[:, 1].astype(jnp.float32)
    lit_real = cos_old * fwd_real - sin_old * fwd_imag
    lit_imag = sin_old * fwd_real + cos_old * fwd_imag
    term_real = cj_real * lit_real - cj_imag * lit_imag
    term_imag = cj_real * lit_imag + cj_imag * lit_real
    local_intersection = jnp.stack(
        [jnp.sum(term_real, axis=(1, 2)), jnp.sum(term_imag, axis=(1, 2))], axis=1
    )
    intersections = lax.psum(local_intersection, "tile")
    gradient_part = jnp.sum(
        intersections[:, 0, None, None] * term_imag - intersections[:, 1, None, None] * term_real,
        axis=0,
    )
    scale = 4.0 * full_phase.shape[1] * forward.shape[0] * lax.axis_size("mode")
    half_width = phase.shape[1]
    gradient_full = lax.psum(gradient_part.astype(jnp.bfloat16), "mode").astype(jnp.float32)
    new_full = full_phase - gradient_full / scale
    phase_next = lax.dynamic_slice_in_dim(
        new_full, lax.axis_index("mode") * half_width, half_width, 1
    )
    cos_new = jnp.cos(new_full)
    sin_new = jnp.sin(new_full)
    launched = jnp.stack(
        [cos_new * fwd_real - sin_new * fwd_imag, sin_new * fwd_real + cos_new * fwd_imag], axis=1
    ).astype(jnp.bfloat16)
    forward_middle = column_pass(launched, operators)
    forward_next = row_pass(forward_middle, operators)
    return (phase_next, forward_next)


def solution(mesh):
    placed = (
        P(("design", "mode"), None, "tile", None),
        P(("design", "mode"), None, "tile", None),
        P(("design", "tile"), "mode"),
        P(None, "design", None, None, None),
        P("design", None),
    )
    return jax.shard_map(
        body,
        mesh=mesh,
        in_specs=placed,
        out_specs=(P(("design", "tile"), "mode"), P(("design", "mode"), None, "tile", None)),
        check_vma=False,
    )
```

profile of v0, /device:TPU:0, one launch (start us, length us, event | category | flops | bytes accessed | tf_op | source)
XLA Modules:
  0.0 1371.6 jit_solution(6158530717524008034)
XLA Ops:
  9.0 7.7 fusion.289
  136.3 6.3 pad_maximum_fusion
  177.8 32.6 %copy.144 = bf16[1,2,512,4096]{2,1,0,3:T(2,128)(2,1)S(1)} copy(bf16[1,2,512,4096]{2,3,1,0:T(8,128)(2,1)S(1)} %fusion.109) | data formatting | bytes 16777216 | tf_op jit(solution)/shard_map/concatenate | solution.py:43
  210.5 190.2 %all_to_all.72 = bf16[1,2,512,4096]{2,1,0,3:T(2,128)(2,1)} all-to-all(bf16[1,2,512,4096]{2,1,0,3:T(2,128)(2,1)S(1)} %copy.144), channel_id=1, replica_groups=mesh['design'=2,'tile'=8,'mode'=2] {'tile'}, dimensions={3} | all-to-all | bytes 16777216 | tf_op jit(solution)/shard_map/all_to_all | solution.py:63
  400.7 21.1 %copy.145 = bf16[1,2,512,8,512]{4,2,3,1,0:T(8,128)(2,1)} copy(bf16[1,2,512,8,512]{2,1,4,3,0:T(2,128)(2,1)} %bitcast.853) | data formatting | bytes 16777216 | tf_op jit(solution)/shard_map/all_to_all | solution.py:63
  439.6 37.5 %copy.146 = bf16[1,2,4096,512]{3,1,0,2:T(2,128)(2,1)} copy(bf16[1,2,4096,512]{3,2,1,0:T(8,128)(2,1)S(1)} %fusion.133) | data formatting | bytes 16777216 | tf_op jit(solution)/shard_map/concatenate | solution.py:59
  482.8 22.8 %all-gather.2.cloned.1.call-done = f32[512,4096]{1,0:T(8,128)} async-done(((f32[512,2048]{1,0:T(8,128)}), f32[512,4096]{1,0:T(8,128)}) %all-gather.2.cloned.1.call-update) | async-done | bytes 8388624 | tf_op jit(solution)/shard_map/all_gather | solution.py:87
  505.6 31.9 %fusion.291 = (f32[512,4096]{1,0:T(8,128)}, f32[512,4096]{1,0:T(8,128)}) fusion(f32[512,4096]{1,0:T(8,128)} %all-gather.2.cloned.1.call-done), kind=kLoop, calls=%fused_computation.315 | loop fusion | bytes 25165824 | tf_op jit(solution)/shard_map/sin | solution.py:89
  537.5 126.7 %all-to-all-done.1 = bf16[1,2,4096,512]{3,1,0,2:T(2,128)(2,1)} async-done(((bf16[1,2,4096,512]{3,1,0,2:T(2,128)(2,1)}), bf16[1,2,4096,512]{3,1,0,2:T(2,128)(2,1)}, u32[]{:S(2)}, u32[]{:S(2)}) %all-to-all-start.1) | async-done | bytes 8388640 | tf_op jit(solution)/shard_map/all_to_all | solution.py:65
  664.2 11.4 copy.233
  675.6 13.5 all_to_all.59
  689.1 20.0 %fusion.287 = (f32[]{:T(128)}, f32[512,4096]{1,0:T(8,128)}, f32[]{:T(128)}, f32[512,4096]{1,0:T(8,128)}) fusion(f32[512,4096]{1,0:T(8,128)} %get-tuple-element.16, f32[512,4096]{1,0:T(8,128)} %get-tuple-element.17, bf16[1,2,512,4096]{3,2,1,0:T(8,128)(2,1)} %all_to_all.59, bf16[1,2,512,4096]{3,2,1,0:T(8,128)(2,1)} %param.5), kind=kLoop, calls=%fused_computation.312 | loop fusion | flops 37748736 | bytes 50331656 | tf_op jit(solution)/shard_map/reduce_sum | solution.py:102
  710.5 19.4 %psum.14 = f32[1,2]{1,0:T(1,128)S(1)} all-reduce(f32[1,2]{1,0:T(1,128)S(1)} %pad_maximum_fusion.10), channel_id=1, replica_groups=mesh['design'=2,'tile'=8,'mode'=2] {'tile'}, use_global_device_ids=true, to_apply=%region_2.3 | all-reduce | flops 2 | bytes 16 | tf_op jit(solution)/shard_map/psum | solution.py:104
  730.5 11.2 subtract_convert_fusion
  741.8 25.8 %all-reduce.6.cloned.1.call-done = bf16[512,4096]{1,0:T(8,128)(2,1)} async-done(((bf16[512,4096]{1,0:T(8,128)(2,1)}), bf16[512,4096]{1,0:T(8,128)(2,1)}) %all-reduce.6.cloned.1.call-update) | async-done | bytes 4194320 | tf_op jit(solution)/shard_map/psum | solution.py:111
  767.6 29.0 %fusion.284 = (f32[512,4096]{1,0:T(8,128)S(1)}, f32[512,4096]{1,0:T(8,128)S(1)}) fusion(f32[512,4096]{1,0:T(8,128)} %all-gather.2.cloned.1.call-done, bf16[512,4096]{1,0:T(8,128)(2,1)} %all-reduce.6.cloned.1.call-done), kind=kLoop, calls=%fused_computation.310 | loop fusion | flops 6291456 | bytes 29360128 | tf_op jit(solution)/shard_map/sin | solution.py:117
  796.6 31.5 %fusion.9 = (bf16[1,1,512,4096]{3,2,1,0:T(8,128)(2,1)S(1)}, bf16[1,1,512,4096]{3,2,1,0:T(8,128)(2,1)}) fusion(f32[512,4096]{1,0:T(8,128)S(1)} %get-tuple-element.2, bf16[1,2,512,4096]{3,2,1,0:T(8,128)(2,1)} %param.5, f32[512,4096]{1,0:T(8,128)S(1)} %get-tuple-element.3), kind=kLoop, calls=%fused_computation.58 | loop fusion | flops 20971520 | bytes 33554432 | tf_op jit(solution)/shard_map/stack | solution.py:118
  853.4 32.6 %copy.148 = bf16[1,2,512,4096]{2,1,0,3:T(2,128)(2,1)S(1)} copy(bf16[1,2,512,4096]{2,3,1,0:T(8,128)(2,1)S(1)} %fusion.181) | data formatting | bytes 16777216 | tf_op jit(solution)/shard_map/concatenate | solution.py:43
  886.0 189.2 %all_to_all.73 = bf16[1,2,512,4096]{2,1,0,3:T(2,128)(2,1)} all-to-all(bf16[1,2,512,4096]{2,1,0,3:T(2,128)(2,1)S(1)} %copy.148), channel_id=1, replica_groups=mesh['design'=2,'tile'=8,'mode'=2] {'tile'}, dimensions={3} | all-to-all | bytes 16777216 | tf_op jit(solution)/shard_map/all_to_all | solution.py:63
  1075.2 21.2 %copy.149 = bf16[1,2,512,8,512]{4,2,3,1,0:T(8,128)(2,1)} copy(bf16[1,2,512,8,512]{2,1,4,3,0:T(2,128)(2,1)} %bitcast.855) | data formatting | bytes 16777216 | tf_op jit(solution)/shard_map/all_to_all | solution.py:63
  1114.1 37.5 %copy.150 = bf16[1,2,4096,512]{3,1,0,2:T(2,128)(2,1)} copy(bf16[1,2,4096,512]{3,2,1,0:T(8,128)(2,1)S(1)} %fusion.205) | data formatting | bytes 16777216 | tf_op jit(solution)/shard_map/concatenate | solution.py:59
  1161.5 177.9 %all-to-all-done.3 = bf16[1,2,4096,512]{3,1,0,2:T(2,128)(2,1)} async-done(((bf16[1,2,4096,512]{3,1,0,2:T(2,128)(2,1)}), bf16[1,2,4096,512]{3,1,0,2:T(2,128)(2,1)}, u32[]{:S(2)}, u32[]{:S(2)}) %all-to-all-start.3) | async-done | bytes 8388640 | tf_op jit(solution)/shard_map/all_to_all | solution.py:65
  1339.4 11.4 copy.151
  1350.9 13.4 all_to_all.67
  (290 shorter events, 234.1 us)
Async XLA Ops:
  69.7 9.0 copy-start.12
  81.9 8.2 copy-start.13
  91.2 8.3 copy-start.27
  101.5 4.4 copy-start.28
  104.8 6.3 copy-start.6
  145.2 19.0 %copy-start.33 = (bf16[1,512,2,768]{3,1,2,0:T(8,128)(2,1)}, bf16[1,512,2,768]{3,1,2,0:T(8,128)(2,1)S(1)}, u32[]{:S(2)}) copy-start(bf16[1,512,2,768]{3,1,2,0:T(8,128)(2,1)S(1)} %get-tuple-element.30) | copy-start | bytes 4718596
  145.3 19.0 %copy-start.37 = (bf16[1,512,2,768]{3,1,2,0:T(8,128)(2,1)}, bf16[1,512,2,768]{3,1,2,0:T(8,128)(2,1)S(1)}, u32[]{:S(2)}) copy-start(bf16[1,512,2,768]{3,1,2,0:T(8,128)(2,1)S(1)} %get-tuple-element.31) | copy-start | bytes 4718596
  148.0 18.5 %copy-start.41 = (bf16[1,512,2,768]{3,1,2,0:T(8,128)(2,1)}, bf16[1,512,2,768]{3,1,2,0:T(8,128)(2,1)S(1)}, u32[]{:S(2)}) copy-start(bf16[1,512,2,768]{3,1,2,0:T(8,128)(2,1)S(1)} %get-tuple-element.28) | copy-start | bytes 4718596
  148.0 18.5 %copy-start.45 = (bf16[1,512,2,768]{3,1,2,0:T(8,128)(2,1)}, bf16[1,512,2,768]{3,1,2,0:T(8,128)(2,1)S(1)}, u32[]{:S(2)}) copy-start(bf16[1,512,2,768]{3,1,2,0:T(8,128)(2,1)S(1)} %get-tuple-element.29) | copy-start | bytes 4718596
  150.7 17.6 %copy-start.49 = (bf16[1,512,2,768]{3,1,2,0:T(8,128)(2,1)}, bf16[1,512,2,768]{3,1,2,0:T(8,128)(2,1)S(1)}, u32[]{:S(2)}) copy-start(bf16[1,512,2,768]{3,1,2,0:T(8,128)(2,1)S(1)} %get-tuple-element.26) | copy-start | bytes 4718596
  150.7 17.6 %copy-start.53 = (bf16[1,512,2,768]{3,1,2,0:T(8,128)(2,1)}, bf16[1,512,2,768]{3,1,2,0:T(8,128)(2,1)S(1)}, u32[]{:S(2)}) copy-start(bf16[1,512,2,768]{3,1,2,0:T(8,128)(2,1)S(1)} %get-tuple-element.27) | copy-start | bytes 4718596
  150.8 4.6 copy-start.22
  153.3 16.9 %copy-start.57 = (bf16[1,512,2,768]{3,1,2,0:T(8,128)(2,1)}, bf16[1,512,2,768]{3,1,2,0:T(8,128)(2,1)S(1)}, u32[]{:S(2)}) copy-start(bf16[1,512,2,768]{3,1,2,0:T(8,128)(2,1)S(1)} %get-tuple-element.24) | copy-start | bytes 4718596
  153.3 7.2 slice-start
  155.3 5.8 slice-start.1
  400.7 21.1 %copy-start.31 = (bf16[1,512,2,768]{3,1,2,0:T(8,128)(2,1)S(1)}, bf16[1,512,2,768]{3,1,2,0:T(8,128)(2,1)}, u32[]{:S(2)}) copy-start(bf16[1,512,2,768]{3,1,2,0:T(8,128)(2,1)} %get-tuple-element.33) | copy-start | bytes 4718596
  421.9 4.6 copy-start.38
  477.0 187.2 %all-to-all-start.1 = ((bf16[1,2,4096,512]{3,1,0,2:T(2,128)(2,1)}), bf16[1,2,4096,512]{3,1,0,2:T(2,128)(2,1)}, u32[]{:S(2)}, u32[]{:S(2)}) async-start(bf16[1,2,4096,512]{3,1,0,2:T(2,128)(2,1)} %copy.146), calls=%async_computation.1 | async-start | bytes 16777216 | tf_op jit(solution)/shard_map/all_to_all | solution.py:65
  482.0 23.6 %all-gather.2.cloned.1.call-start = ((), (), s32[]{:S(2)}) async-start(), calls=%async_computation.4 | async-start | bytes 12582912 | tf_op jit(solution)/shard_map/all_gather | solution.py:87
  482.8 284.9 %all-reduce.6.cloned.1.call-start = ((), (), s32[]{:S(2)}) async-start(), calls=%async_computation.5 | async-start | bytes 8388608 | tf_op jit(solution)/shard_map/psum | solution.py:111
  796.6 31.5 %copy-start = (f32[512,4096]{1,0:T(8,128)}, f32[512,4096]{1,0:T(8,128)S(1)}, u32[]{:S(2)}) copy-start(f32[512,4096]{1,0:T(8,128)S(1)} %get-tuple-element.3) | copy-start | bytes 25165828
  1075.2 21.2 %copy-start.32 = (bf16[1,512,2,768]{3,1,2,0:T(8,128)(2,1)S(1)}, bf16[1,512,2,768]{3,1,2,0:T(8,128)(2,1)}, u32[]{:S(2)}) copy-start(bf16[1,512,2,768]{3,1,2,0:T(8,128)(2,1)} %get-tuple-element.33) | copy-start | bytes 4718596
  1096.4 4.6 copy-start.40
  1151.6 187.9 %all-to-all-start.3 = ((bf16[1,2,4096,512]{3,1,0,2:T(2,128)(2,1)}), bf16[1,2,4096,512]{3,1,0,2:T(2,128)(2,1)}, u32[]{:S(2)}, u32[]{:S(2)}) async-start(bf16[1,2,4096,512]{3,1,0,2:T(2,128)(2,1)} %copy.150), calls=%async_computation.3 | async-start | bytes 16777216 | tf_op jit(solution)/shard_map/all_to_all | solution.py:65
  (73 other events, 170.2 us)
Sparse Core Ops, SparseCore 0:
  484.4 21.1 all-gather.1
  741.9 25.6 all-reduce.5
where the time goes:
time: 1380 us; the launch traced here: 1370 us
  blocking collectives  399 us (29%)
  waiting for transfers between devices  354 us (26%)
  local copies, waits for them, and re-layouts  345 us (25%)
  other arithmetic  136 us (10%)
  matrix products  112 us (8%)
  between operations  15.4 us (1%)
    all_to_all x2, blocking collectives, row_pass(): lax.all_to_all(middle, 'tile', split_axis=3, concat_axis=2, tiled=True)  379 us
    all_to_all x2, waiting for transfers between devices, row_pass(): lax.all_to_all(finished, 'tile', split_axis=2, concat_axis=3, tiled=True)  305 us
    concatenate x2, local copies, waits for them, and re-layouts, whole_row_pass(): return jnp.concatenate(results, axis=2)  74.9 us
    concatenate x2, local copies, waits for them, and re-layouts, column_pass(): return jnp.concatenate(results, axis=3)  65.3 us
    all_to_all x4, local copies, waits for them, and re-layouts, row_pass(): lax.all_to_all(finished, 'tile', split_axis=2, concat_axis=3, tiled=True)  49.7 us
    all_to_all x2, local copies, waits for them, and re-layouts, row_pass(): lax.all_to_all(middle, 'tile', split_axis=3, concat_axis=2, tiled=True)  42.3 us
    another operation x2, other arithmetic, body(): jnp.stack([cos_new * fwd_real - sin_new * fwd_imag, sin_new * fwd_real +...  37.8 us
    sin x1, local copies, waits for them, and re-layouts, body(): sin_old = jnp.sin(full_phase)  31.9 us
  transfers between devices with their start and end apart: 4, of which 4 were waited for; matrix products, arithmetic and copies ran while one was open for 3% of the time, Pallas kernels for 0%

commit v1 on v0

--- a/solution.py
+++ b/solution.py
@@ -1,3 +1,4 @@
+import functools
 import jax
 import jax.numpy as jnp
 from jax import lax
@@ -5,6 +6,18 @@
 
 BLK = 64
 RADIUS = 2
+
+
+def works_pack(sheet, axis_no, pos_dim):
+    return jnp.concatenate(
+        lax.all_to_all(
+            jnp.stack(jnp.split(sheet, lax.axis_size("tile"), axis=axis_no), axis=0), "tile", 0, 0
+        ),
+        pos_dim,
+    )
+
+
+_supply_all_scales = functools.partial(works_pack, axis_no=2, pos_dim=3)
 
 
 def dense_operator(blocks_re, blocks_im, shifts, in_blocks):
@@ -62,7 +75,7 @@
 def row_pass(middle, operators):
     columns = lax.all_to_all(middle, "tile", split_axis=3, concat_axis=2, tiled=True)
     finished = whole_row_pass(columns, operators)
-    return lax.all_to_all(finished, "tile", split_axis=2, concat_axis=3, tiled=True)
+    return _supply_all_scales(finished)
 
 
 def body(forward, adjoint_next, phase, blocks, offsets):

time: 1380 us -> 1330 us (0.964)
  local copies, waits for them, and re-layouts: 345 us -> 272 us
  matrix products: 112 us -> 128 us
    concatenate x2 -> x0, local copies, waits for them, and re-layouts: 74.9 us -> none  [whole_row_pass(): return jnp.concatenate(results, axis=2)]
    all_to_all x4 -> x0, local copies, waits for them, and re-layouts: 49.7 us -> none  [row_pass(): lax.all_to_all(finished, 'tile', split_axis=2, concat_axis=3, tiled=True)]
    sin x1 -> x0, local copies, waits for them, and re-layouts: 31.9 us -> none  [body(): sin_old = jnp.sin(full_phase)]
    cos x0 -> x1, local copies, waits for them, and re-layouts: none -> 31.5 us  [body(): cos_old = jnp.cos(full_phase)]
    reshape x0 -> x2, local copies, waits for them, and re-layouts: none -> 23.7 us  [works_pack(): jnp.concatenate(lax.all_to_all(jnp.stack(jnp.split(sheet, lax.axis_size('...]
    unnamed x186 -> x189, local copies, waits for them, and re-layouts: 15.8 us -> 38.5 us
    dot_general x16, matrix products: 31.5 us -> 47.4 us  [whole_row_pass(): jnp.einsum('mpjw,qipj->mqiw', window, operator, preferred_element_type=jn...]
where the time goes in v1:
time: 1330 us; the launch traced here: 1320 us
  blocking collectives  399 us (30%)
  waiting for transfers between devices  354 us (27%)
  local copies, waits for them, and re-layouts  272 us (20%)
  other arithmetic  138 us (10%)
  matrix products  128 us (10%)
  between operations  15 us (1%)
    all_to_all x2, blocking collectives, row_pass(): lax.all_to_all(middle, 'tile', split_axis=3, concat_axis=2, tiled=True)  379 us
    all_to_all x2, waiting for transfers between devices, works_pack(): lax.all_to_all(jnp.stack(jnp.split(sheet, lax.axis_size('tile'), axis=axi...  305 us
    concatenate x2, local copies, waits for them, and re-layouts, column_pass(): return jnp.concatenate(results, axis=3)  65.3 us
    dot_general x16, matrix products, whole_row_pass(): jnp.einsum('mpjw,qipj->mqiw', window, operator, preferred_element_type=jn...  47.4 us
    all_to_all x2, local copies, waits for them, and re-layouts, row_pass(): lax.all_to_all(middle, 'tile', split_axis=3, concat_axis=2, tiled=True)  42.3 us
    unnamed x189, local copies, waits for them, and re-layouts  38.5 us
    another operation x2, other arithmetic, body(): jnp.stack([cos_new * fwd_real - sin_new * fwd_imag, sin_new * fwd_real +...  38 us
    dot_general x16, matrix products, column_pass(): jnp.einsum('mprj,qipj->mqri', window, operator, preferred_element_type=jn...  31.5 us
  transfers between devices with their start and end apart: 4, of which 4 were waited for; matrix products, arithmetic and copies ran while one was open for 3% of the time, Pallas kernels for 0%

profile of v1, /device:TPU:0, one launch (start us, length us, event | category | flops | bytes accessed | tf_op | source)
XLA Modules:
  0.0 1316.5 jit_solution(6090470897520775205)
XLA Ops:
  9.0 7.7 fusion.291
  136.4 6.3 pad_maximum_fusion
  177.9 32.6 %copy.145 = bf16[1,2,512,4096]{2,1,0,3:T(2,128)(2,1)S(1)} copy(bf16[1,2,512,4096]{2,3,1,0:T(8,128)(2,1)S(1)} %fusion.109) | data formatting | bytes 16777216 | tf_op jit(solution)/shard_map/concatenate | solution.py:56
  210.5 190.2 %all_to_all.46 = bf16[1,2,512,4096]{2,1,0,3:T(2,128)(2,1)} all-to-all(bf16[1,2,512,4096]{2,1,0,3:T(2,128)(2,1)S(1)} %copy.145), channel_id=1, replica_groups=mesh['design'=2,'tile'=8,'mode'=2] {'tile'}, dimensions={3} | all-to-all | bytes 16777216 | tf_op jit(solution)/shard_map/all_to_all | solution.py:76
  400.8 21.1 %copy.146 = bf16[1,2,512,8,512]{4,2,3,1,0:T(8,128)(2,1)} copy(bf16[1,2,512,8,512]{2,1,4,3,0:T(2,128)(2,1)} %bitcast.837) | data formatting | bytes 16777216 | tf_op jit(solution)/shard_map/all_to_all | solution.py:76
  452.4 22.8 %all-gather.2.cloned.1.call-done = f32[512,4096]{1,0:T(8,128)} async-done(((f32[512,2048]{1,0:T(8,128)}), f32[512,4096]{1,0:T(8,128)}) %all-gather.2.cloned.1.call-update) | async-done | bytes 8388624 | tf_op jit(solution)/shard_map/all_gather | solution.py:100
  475.2 31.5 %fusion.289 = (f32[512,4096]{1,0:T(8,128)}, f32[512,4096]{1,0:T(8,128)}) fusion(f32[512,4096]{1,0:T(8,128)} %all-gather.2.cloned.1.call-done), kind=kLoop, calls=%fused_computation.310 | loop fusion | bytes 25165824 | tf_op jit(solution)/shard_map/cos | solution.py:101
  506.7 127.1 %all-to-all-done.1 = bf16[8,1,2,512,512]{4,3,2,1,0:T(8,128)(2,1)} async-done(((bf16[8,1,2,512,512]{4,3,2,1,0:T(8,128)(2,1)}), bf16[8,1,2,512,512]{4,3,2,1,0:T(8,128)(2,1)}, u32[]{:S(2)}, u32[]{:S(2)}) %all-to-all-start.1) | async-done | bytes 8388640 | tf_op jit(solution)/shard_map/all_to_all | solution.py:13
  633.8 11.8 copy.147
  651.5 6.4 copy.212
  658.0 6.3 copy.213
  664.3 19.9 %fusion.269 = (f32[]{:T(128)}, f32[]{:T(128)}, f32[512,4096]{1,0:T(8,128)}, f32[512,4096]{1,0:T(8,128)}) fusion(bf16[1,1,512,4096]{3,2,1,0:T(8,128)(2,1)} %copy.213, bf16[1,1,512,4096]{3,2,1,0:T(8,128)(2,1)} %copy.212, f32[512,4096]{1,0:T(8,128)} %get-tuple-element.15, bf16[1,2,512,4096]{3,2,1,0:T(8,128)(2,1)} %param.5, f32[512,4096]{1,0:T(8,128)} %get-tuple-element.14), kind=kLoop, calls=%fused_computation.308 | loop fusion | flops 37748736 | bytes 50331656 | tf_op jit(solution)/shard_map/reduce_sum | solution.py:115
  685.5 19.4 %psum.14 = f32[1,2]{1,0:T(1,128)S(1)} all-reduce(f32[1,2]{1,0:T(1,128)S(1)} %pad_maximum_fusion.10), channel_id=1, replica_groups=mesh['design'=2,'tile'=8,'mode'=2] {'tile'}, use_global_device_ids=true, to_apply=%region_2.3 | all-reduce | flops 2 | bytes 16 | tf_op jit(solution)/shard_map/psum | solution.py:117
  705.6 13.2 %subtract_convert_fusion = bf16[512,4096]{1,0:T(8,128)(2,1)} fusion(f32[]{:T(128)} %bitcast.163, f32[]{:T(128)} %bitcast.162, f32[512,4096]{1,0:T(8,128)} %get-tuple-element.10, bf16[1,1,512,4096]{3,2,1,0:T(8,128)(2,1)} %copy.213, f32[512,4096]{1,0:T(8,128)} %get-tuple-element.11, bf16[1,1,512,4096]{3,2,1,0:T(8,128)(2,1)} %copy.212), kind=kLoop, calls=%fused_computation.47 | loop fusion | flops 25165824 | bytes 29360136 | tf_op jit(solution)/shard_map/convert_element_type | solution.py:124
  718.8 25.9 %all-reduce.6.cloned.1.call-done = bf16[512,4096]{1,0:T(8,128)(2,1)} async-done(((bf16[512,4096]{1,0:T(8,128)(2,1)}), bf16[512,4096]{1,0:T(8,128)(2,1)}) %all-reduce.6.cloned.1.call-update) | async-done | bytes 4194320 | tf_op jit(solution)/shard_map/psum | solution.py:124
  744.6 29.0 %fusion.286 = (f32[512,4096]{1,0:T(8,128)S(1)}, f32[512,4096]{1,0:T(8,128)S(1)}) fusion(f32[512,4096]{1,0:T(8,128)} %all-gather.2.cloned.1.call-done, bf16[512,4096]{1,0:T(8,128)(2,1)} %all-reduce.6.cloned.1.call-done), kind=kLoop, calls=%fused_computation.309 | loop fusion | flops 6291456 | bytes 29360128 | tf_op jit(solution)/shard_map/sin | solution.py:130
  773.6 31.7 %fusion.9 = (bf16[1,1,512,4096]{3,2,1,0:T(8,128)(2,1)S(1)}, bf16[1,1,512,4096]{3,2,1,0:T(8,128)(2,1)}) fusion(f32[512,4096]{1,0:T(8,128)S(1)} %get-tuple-element.8, bf16[1,2,512,4096]{3,2,1,0:T(8,128)(2,1)} %param.5, f32[512,4096]{1,0:T(8,128)S(1)} %get-tuple-element.9), kind=kLoop, calls=%fused_computation.57 | loop fusion | flops 20971520 | bytes 33554432 | tf_op jit(solution)/shard_map/stack | solution.py:131
  805.3 6.3 pad_maximum_fusion.1
  830.6 32.6 %copy.150 = bf16[1,2,512,4096]{2,1,0,3:T(2,128)(2,1)S(1)} copy(bf16[1,2,512,4096]{2,3,1,0:T(8,128)(2,1)S(1)} %fusion.181) | data formatting | bytes 16777216 | tf_op jit(solution)/shard_map/concatenate | solution.py:56
  863.2 189.2 %all_to_all.47 = bf16[1,2,512,4096]{2,1,0,3:T(2,128)(2,1)} all-to-all(bf16[1,2,512,4096]{2,1,0,3:T(2,128)(2,1)S(1)} %copy.150), channel_id=1, replica_groups=mesh['design'=2,'tile'=8,'mode'=2] {'tile'}, dimensions={3} | all-to-all | bytes 16777216 | tf_op jit(solution)/shard_map/all_to_all | solution.py:76
  1052.4 21.2 %copy.151 = bf16[1,2,512,8,512]{4,2,3,1,0:T(8,128)(2,1)} copy(bf16[1,2,512,8,512]{2,1,4,3,0:T(2,128)(2,1)} %bitcast.838) | data formatting | bytes 16777216 | tf_op jit(solution)/shard_map/all_to_all | solution.py:76
  1107.7 178.0 %all-to-all-done.3 = bf16[8,1,2,512,512]{4,3,2,1,0:T(8,128)(2,1)} async-done(((bf16[8,1,2,512,512]{4,3,2,1,0:T(8,128)(2,1)}), bf16[8,1,2,512,512]{4,3,2,1,0:T(8,128)(2,1)}, u32[]{:S(2)}, u32[]{:S(2)}) %all-to-all-start.3) | async-done | bytes 8388640 | tf_op jit(solution)/shard_map/all_to_all | solution.py:13
  1285.7 11.9 copy.152
  1297.6 11.9 copy.153
  (290 shorter events, 247.4 us)
Async XLA Ops:
  69.7 9.0 copy-start.12
  81.8 8.1 copy-start.13
  91.2 8.3 copy-start.27
  101.5 4.4 copy-start.28
  104.8 6.3 copy-start.6
  145.3 19.1 %copy-start.33 = (bf16[1,512,2,768]{3,1,2,0:T(8,128)(2,1)}, bf16[1,512,2,768]{3,1,2,0:T(8,128)(2,1)S(1)}, u32[]{:S(2)}) copy-start(bf16[1,512,2,768]{3,1,2,0:T(8,128)(2,1)S(1)} %get-tuple-element.34) | copy-start | bytes 4718596
  145.3 19.1 %copy-start.37 = (bf16[1,512,2,768]{3,1,2,0:T(8,128)(2,1)}, bf16[1,512,2,768]{3,1,2,0:T(8,128)(2,1)S(1)}, u32[]{:S(2)}) copy-start(bf16[1,512,2,768]{3,1,2,0:T(8,128)(2,1)S(1)} %get-tuple-element.35) | copy-start | bytes 4718596
  148.0 18.5 %copy-start.41 = (bf16[1,512,2,768]{3,1,2,0:T(8,128)(2,1)}, bf16[1,512,2,768]{3,1,2,0:T(8,128)(2,1)S(1)}, u32[]{:S(2)}) copy-start(bf16[1,512,2,768]{3,1,2,0:T(8,128)(2,1)S(1)} %get-tuple-element.32) | copy-start | bytes 4718596
  148.0 18.5 %copy-start.45 = (bf16[1,512,2,768]{3,1,2,0:T(8,128)(2,1)}, bf16[1,512,2,768]{3,1,2,0:T(8,128)(2,1)S(1)}, u32[]{:S(2)}) copy-start(bf16[1,512,2,768]{3,1,2,0:T(8,128)(2,1)S(1)} %get-tuple-element.33) | copy-start | bytes 4718596
  150.8 17.6 %copy-start.49 = (bf16[1,512,2,768]{3,1,2,0:T(8,128)(2,1)}, bf16[1,512,2,768]{3,1,2,0:T(8,128)(2,1)S(1)}, u32[]{:S(2)}) copy-start(bf16[1,512,2,768]{3,1,2,0:T(8,128)(2,1)S(1)} %get-tuple-element.30) | copy-start | bytes 4718596
  150.8 17.6 %copy-start.53 = (bf16[1,512,2,768]{3,1,2,0:T(8,128)(2,1)}, bf16[1,512,2,768]{3,1,2,0:T(8,128)(2,1)S(1)}, u32[]{:S(2)}) copy-start(bf16[1,512,2,768]{3,1,2,0:T(8,128)(2,1)S(1)} %get-tuple-element.31) | copy-start | bytes 4718596
  150.8 4.5 copy-start.22
  153.3 16.9 %copy-start.57 = (bf16[1,512,2,768]{3,1,2,0:T(8,128)(2,1)}, bf16[1,512,2,768]{3,1,2,0:T(8,128)(2,1)S(1)}, u32[]{:S(2)}) copy-start(bf16[1,512,2,768]{3,1,2,0:T(8,128)(2,1)S(1)} %get-tuple-element.28) | copy-start | bytes 4718596
  153.3 7.2 slice-start
  155.3 5.9 slice-start.1
  400.8 21.1 %copy-start.31 = (bf16[1,512,2,768]{3,1,2,0:T(8,128)(2,1)S(1)}, bf16[1,512,2,768]{3,1,2,0:T(8,128)(2,1)}, u32[]{:S(2)}) copy-start(bf16[1,512,2,768]{3,1,2,0:T(8,128)(2,1)} %get-tuple-element.37) | copy-start | bytes 4718596
  421.9 5.0 copy-start.38
  446.5 187.4 %all-to-all-start.1 = ((bf16[8,1,2,512,512]{4,3,2,1,0:T(8,128)(2,1)}), bf16[8,1,2,512,512]{4,3,2,1,0:T(8,128)(2,1)}, u32[]{:S(2)}, u32[]{:S(2)}) async-start(bf16[8,1,2,512,512]{4,3,2,1,0:T(8,128)(2,1)} %fusion.133), calls=%async_computation.1 | async-start | bytes 16777216 | tf_op jit(solution)/shard_map/all_to_all | solution.py:13
  451.6 23.6 %all-gather.2.cloned.1.call-start = ((), (), s32[]{:S(2)}) async-start(), calls=%async_computation.4 | async-start | bytes 12582912 | tf_op jit(solution)/shard_map/all_gather | solution.py:100
  452.4 292.2 %all-reduce.6.cloned.1.call-start = ((), (), s32[]{:S(2)}) async-start(), calls=%async_computation.5 | async-start | bytes 8388608 | tf_op jit(solution)/shard_map/psum | solution.py:124
  773.6 31.7 %copy-start = (f32[512,4096]{1,0:T(8,128)}, f32[512,4096]{1,0:T(8,128)S(1)}, u32[]{:S(2)}) copy-start(f32[512,4096]{1,0:T(8,128)S(1)} %get-tuple-element.9) | copy-start | bytes 25165828
  1052.4 21.2 %copy-start.32 = (bf16[1,512,2,768]{3,1,2,0:T(8,128)(2,1)S(1)}, bf16[1,512,2,768]{3,1,2,0:T(8,128)(2,1)}, u32[]{:S(2)}) copy-start(bf16[1,512,2,768]{3,1,2,0:T(8,128)(2,1)} %get-tuple-element.37) | copy-start | bytes 4718596
  1073.5 5.0 copy-start.40
  1098.1 187.6 %all-to-all-start.3 = ((bf16[8,1,2,512,512]{4,3,2,1,0:T(8,128)(2,1)}), bf16[8,1,2,512,512]{4,3,2,1,0:T(8,128)(2,1)}, u32[]{:S(2)}, u32[]{:S(2)}) async-start(bf16[8,1,2,512,512]{4,3,2,1,0:T(8,128)(2,1)} %fusion.205), calls=%async_computation.3 | async-start | bytes 16777216 | tf_op jit(solution)/shard_map/all_to_all | solution.py:13
  (73 other events, 194.2 us)
Sparse Core Ops, SparseCore 0:
  454.0 21.1 all-gather.1
  718.9 25.6 all-reduce.5
